TPU v7x, 32 devices: a whole 2x2x4 slice. The times are simulated.
32 devices in a mesh: row: 16 (over z, x, core), col: 2 (over y).
Axes of the slice: x: 2, y: 2, z: 4, core: 2. Of those that a mesh axis runs over, the one named last changes fastest.
Arguments:
- matrix_panel: bfloat16 [128, 131072], P('col', 'row'), may hold values from -6 to 6
- row_signs: int32 [131072], P('row'), may hold values from -1 to 1, as said below
- sample_rows: int32 [2048], replicated, may hold values from 0 to 131071, as said below
Outputs:
- sketch: float32 [128, 2048], P('col', 'row')
- gram: float32 [128, 128], P('col')
Inputs may be any that keep to these rules, and one draw needn't show every extreme that they name: `row_signs`: each entry is -1 or +1. `sample_rows`: strictly increasing, so all distinct.
All inputs are finite; a program needn't handle non-finite values.
Results may differ from a plain program's by a relative error of at most 0.0003.
Values sent between devices are 32-bit elements; how exact they have to be, the bound alone decides.
No kernel may reach another device: no remote copies, remote signals or barrier semaphores. Data moves between devices by JAX's collectives and lax.ppermute only.
A program may use at most 64 MiB of HBM per device.

v0:
```python
import jax
import jax.numpy as jnp
from jax import lax
from jax.sharding import PartitionSpec as P


def parity_sign(left, right, bit_count):
    common = jnp.bitwise_and(left, right)
    total = jnp.zeros_like(common)
    for bit_index in range(bit_count):
        total = total + jnp.bitwise_and(jnp.right_shift(common, bit_index), 1)
    return (1 - 2 * jnp.bitwise_and(total, 1)).astype(jnp.float32)


def hadamard(order_size):
    bit_count = order_size.bit_length() - 1
    row_index = jnp.arange(order_size, dtype=jnp.int32)
    return parity_sign(row_index[:, None], row_index[None, :], bit_count)


def local_mix(block, signs):
    columns, length = block.shape
    first_size = min(length, 256)
    second_size = length // first_size
    values = block.astype(jnp.float32) * signs.astype(jnp.float32)[None, :]
    values = values.reshape(columns, first_size, second_size)
    values = jnp.einsum(
        "cab,ad->cdb", values, hadamard(first_size), precision=lax.Precision.HIGHEST
    )
    values = jnp.einsum(
        "cdb,be->cde", values, hadamard(second_size), precision=lax.Precision.HIGHEST
    )
    return values.reshape(columns, length) / jnp.sqrt(jnp.float32(length))


def body(matrix_panel, row_signs, sample_rows):
    devices = lax.axis_size("row")
    position = lax.axis_index("row")
    bit_count = devices.bit_length() - 1
    columns, length = matrix_panel.shape
    everything = sample_rows.shape[0]
    per_device = everything // devices
    mixed = local_mix(matrix_panel, row_signs)
    owner = sample_rows // length
    offset = sample_rows - owner * length
    chosen = jnp.take(mixed, offset, axis=1)
    pieces = chosen.reshape(columns, devices, per_device)
    received = lax.all_to_all(pieces, "row", split_axis=1, concat_axis=1, tiled=True)
    mine = lax.dynamic_slice_in_dim(owner, position * per_device, per_device, 0)
    sources = jnp.arange(devices, dtype=jnp.int32)
    table = parity_sign(sources[:, None], mine[None, :], bit_count)
    summed = jnp.sum(received * table[None, :, :], axis=1)
    sketch = summed / jnp.sqrt(jnp.float32(devices))
    gathered = lax.all_gather(sketch, "col", axis=0, tiled=True)
    partial_gram = jnp.dot(gathered, gathered.T, precision=lax.Precision.HIGHEST)
    totals = lax.psum(partial_gram, "row")
    own_rows = lax.dynamic_slice_in_dim(totals, lax.axis_index("col") * columns, columns, 0)
    gram = own_rows / everything
    return (sketch, gram)


def solution(mesh):
    return jax.shard_map(
        body,
        mesh=mesh,
        in_specs=(P("col", "row"), P("row"), P()),
        out_specs=(P("col", "row"), P("col", None)),
        check_vma=False,
    )
```

profile of v0, /device:TPU:8, one launch (start us, length us, event | category | flops | bytes accessed | tf_op | source)
XLA Modules:
  0.0 157.8 jit_solution(18320951381184153002)
XLA Ops:
  7.2 0.7 add_select_fusion
  7.9 0.7 and_bitcast_fusion
  8.6 0.8 convert_element_type.21
  9.4 1.4 convert_multiply_fusion
  10.8 2.7 %copy.13 = f32[64,8192]{0,1:T(8,128)} copy(f32[64,8192]{1,0:T(8,128)S(1)} %convert_multiply_fusion) | data formatting | bytes 4194304 | tf_op jit(solution)/shard_map/mul | solution.py:25
  13.5 4.5 %copy.14 = f32[64,256,32]{1,2,0:T(8,128)S(1)} copy(f32[64,256,32]{0,2,1:T(8,128)} %bitcast.21) | data formatting | bytes 4194304 | tf_op jit(solution)/shard_map/reshape | solution.py:26
  17.9 2.2 %fusion = f32[256,2048]{0,1:S(1)} fusion(f32[256,2048]{0,1:T(8,128)S(1)} %bitcast.22), kind=kOutput, calls=%fused_computation.5 | convolution fusion | flops 1612447744 | bytes 4194304
  20.1 1.9 %convolution_multiply_fusion = f32[64,256,32]{1,2,0:T(8,128)S(1)} fusion(f32[64,256,32]{1,2,0:T(8,128)S(1)} %bitcast.23), kind=kOutput, calls=%fused_computation.2 | convolution fusion | flops 201870336 | bytes 4194304 | tf_op jit(solution)/shard_map/cdb,be->cde/dot_general | solution.py:30
  22.0 4.5 %copy.15 = f32[64,256,32]{0,2,1:T(8,128)} copy(f32[64,256,32]{1,2,0:T(8,128)S(1)} %convolution_multiply_fusion) | data formatting | bytes 4194304 | tf_op jit(solution)/shard_map/div | solution.py:33
  26.5 7.6 %gather_fusion = f32[2048,64]{1,0:T(8,128)S(1)} fusion(f32[64,8192]{0,1:T(8,128)} %bitcast.20, s32[2048]{0:T(1024)S(1)} %get-tuple-element.7), kind=kCustom, calls=%fused_computation | custom fusion | bytes 1056768 | tf_op jit(solution)/shard_map/jit(_take)/gather | solution.py:46
  34.2 0.3 copy.16
  34.5 0.8 broadcast_select_fusion
  35.3 6.3 %all-to-all-start = ((f32[64,16,128]{2,0,1:T(8,128)}), f32[64,16,128]{2,0,1:T(8,128)S(1)}, u32[]{:S(2)}, u32[]{:S(2)}) async-start(f32[64,16,128]{2,0,1:T(8,128)} %broadcast_select_fusion), calls=%async_computation | async-start | bytes 1048576 | tf_op jit(solution)/shard_map/all_to_all | solution.py:48
  41.6 0.0 all-reduce.2.cloned.1.call-start
  41.7 0.1 dynamic_slice.6
  41.8 13.3 %all-to-all-done = f32[64,16,128]{2,0,1:T(8,128)S(1)} async-done(((f32[64,16,128]{2,0,1:T(8,128)}), f32[64,16,128]{2,0,1:T(8,128)S(1)}, u32[]{:S(2)}, u32[]{:S(2)}) %all-to-all-start) | async-done | bytes 524320 | tf_op jit(solution)/shard_map/all_to_all | solution.py:48
  55.1 0.1 copy.20
  55.2 0.1 copy.19
  55.3 0.0 copy-start
  55.3 4.7 %all_gather.3 = f32[128,128]{1,0:T(8,128)S(1)} all-gather(f32[64,128]{1,0:T(8,128)S(1)} %copy.19), channel_id=1, replica_groups=mesh['row'=16,'col'=2] {'col'}, dimensions={0}, use_global_device_ids=true | all-gather | bytes 98304 | tf_op jit(solution)/shard_map/all_gather | solution.py:54
  60.0 0.9 fusion.81
  60.9 0.0 all-reduce.2.cloned.1.call-update
  61.0 88.7 %all-reduce.2.cloned.1.call-done = f32[128,128]{1,0:T(8,128)} async-done(((f32[128,128]{1,0:T(8,128)}), f32[128,128]{1,0:T(8,128)}) %all-reduce.2.cloned.1.call-update) | async-done | bytes 65552 | tf_op jit(solution)/shard_map/psum | solution.py:56
  149.6 1.4 dynamic-slice_multiply_fusion
  151.0 0.0 copy-done
  (3 shorter events, 0.1 us)
Async XLA Ops:
  35.3 19.8 %all-to-all-start = ((f32[64,16,128]{2,0,1:T(8,128)}), f32[64,16,128]{2,0,1:T(8,128)S(1)}, u32[]{:S(2)}, u32[]{:S(2)}) async-start(f32[64,16,128]{2,0,1:T(8,128)} %broadcast_select_fusion), calls=%async_computation | async-start | bytes 1048576 | tf_op jit(solution)/shard_map/all_to_all | solution.py:48
  41.6 108.0 %all-reduce.2.cloned.1.call-start = ((), (), s32[]{:S(2)}) async-start(), calls=%async_computation.1 | async-start | bytes 131072 | tf_op jit(solution)/shard_map/psum | solution.py:56
  55.3 95.7 %copy-start = (f32[64,128]{1,0:T(8,128)}, f32[64,128]{1,0:T(8,128)S(1)}, u32[]{:S(2)}) copy-start(f32[64,128]{1,0:T(8,128)S(1)} %copy.19) | copy-start | bytes 98308
Sparse Core Ops, SparseCore 0:
  61.1 88.5 all-reduce.1
where the time goes:
time: 158 us
  waiting for transfers between devices  102 us (65%)
  local copies, waits for them, and re-layouts  19.9 us (13%)
  between operations  14.1 us (9%)
  starting transfers between devices  6.3 us (4%)
  other arithmetic  5.87 us (4%)
  matrix products  4.98 us (3%)
  blocking collectives  4.71 us (3%)
    psum x1, waiting for transfers between devices, body(): totals = lax.psum(partial_gram, 'row')  88.7 us
    all_to_all x1, waiting for transfers between devices, body(): lax.all_to_all(pieces, 'row', split_axis=1, concat_axis=1, tiled=True)  13.3 us
    gather x2, local copies, waits for them, and re-layouts, body(): chosen = jnp.take(mixed, offset, axis=1)  7.96 us
    all_to_all x1, starting transfers between devices, body(): lax.all_to_all(pieces, 'row', split_axis=1, concat_axis=1, tiled=True)  6.27 us
    all_gather x1, blocking collectives, body(): gathered = lax.all_gather(sketch, 'col', axis=0, tiled=True)  4.71 us
    div x1, local copies, waits for them, and re-layouts, local_mix(): return values.reshape(columns, length) / jnp.sqrt(jnp.float32(length))  4.48 us
    reshape x1, local copies, waits for them, and re-layouts, local_mix(): values = values.reshape(columns, first_size, second_size)  4.46 us
  transfers between devices with their start and end apart: 2, of which 2 were waited for; matrix products, arithmetic and copies ran while one was open for 0% of the time, Pallas kernels for 0%

commit v1 on v0

--- a/solution.py
+++ b/solution.py
@@ -53,7 +53,8 @@
     sketch = summed / jnp.sqrt(jnp.float32(devices))
     gathered = lax.all_gather(sketch, "col", axis=0, tiled=True)
     partial_gram = jnp.dot(gathered, gathered.T, precision=lax.Precision.HIGHEST)
-    totals = lax.psum(partial_gram, "row")
+    shards = lax.all_gather(partial_gram, "row")
+    totals = jnp.sum(shards, axis=0)
     own_rows = lax.dynamic_slice_in_dim(totals, lax.axis_index("col") * columns, columns, 0)
     gram = own_rows / everything
     return (sketch, gram)

time: 158 us -> 109 us (0.69)
  the two profiles are of different devices: /device:TPU:8 before, /device:TPU:0 now
where the time goes in v1:
time: 109 us
  waiting for transfers between devices  51.6 us (47%)
  local copies, waits for them, and re-layouts  19.9 us (18%)
  between operations  14.1 us (13%)
  starting transfers between devices  7.43 us (7%)
  other arithmetic  6.4 us (6%)
  matrix products  4.98 us (5%)
  blocking collectives  4.58 us (4%)
    all_gather x1, waiting for transfers between devices, body(): shards = lax.all_gather(partial_gram, 'row')  37.5 us
    all_to_all x1, waiting for transfers between devices, body(): lax.all_to_all(pieces, 'row', split_axis=1, concat_axis=1, tiled=True)  14.1 us
    gather x2, local copies, waits for them, and re-layouts, body(): chosen = jnp.take(mixed, offset, axis=1)  7.96 us
    all_to_all x1, starting transfers between devices, body(): lax.all_to_all(pieces, 'row', split_axis=1, concat_axis=1, tiled=True)  7.39 us
    all_gather x1, blocking collectives, body(): gathered = lax.all_gather(sketch, 'col', axis=0, tiled=True)  4.58 us
    div x1, local copies, waits for them, and re-layouts, local_mix(): return values.reshape(columns, length) / jnp.sqrt(jnp.float32(length))  4.48 us
    reshape x1, local copies, waits for them, and re-layouts, local_mix(): values = values.reshape(columns, first_size, second_size)  4.47 us
    mul x1, local copies, waits for them, and re-layouts, local_mix(): values = block.astype(jnp.float32) * signs.astype(jnp.float32)[None, :]  2.7 us
  transfers between devices with their start and end apart: 2, of which 2 were waited for; matrix products, arithmetic and copies ran while one was open for 0% of the time, Pallas kernels for 0%

profile of v1, /device:TPU:0, one launch (start us, length us, event | category | flops | bytes accessed | tf_op | source)
XLA Modules:
  0.0 109.0 jit_solution(8613918768650917385)
XLA Ops:
  7.2 0.7 add_select_fusion
  7.9 0.7 and_bitcast_fusion
  8.6 0.8 convert_element_type.21
  9.4 1.4 %convert_multiply_fusion = f32[64,8192]{1,0:T(8,128)S(1)} fusion(bf16[64,8192]{1,0:T(8,128)(2,1)} %param.3, f32[8192]{0:T(1024)S(1)} %convert_element_type.21), kind=kLoop, calls=%fused_computation.1 | loop fusion | flops 1048576 | bytes 3178496 | tf_op jit(solution)/shard_map/mul | solution.py:25
  10.8 2.7 %copy.13 = f32[64,8192]{0,1:T(8,128)} copy(f32[64,8192]{1,0:T(8,128)S(1)} %convert_multiply_fusion) | data formatting | bytes 4194304 | tf_op jit(solution)/shard_map/mul | solution.py:25
  13.5 4.5 %copy.14 = f32[64,256,32]{1,2,0:T(8,128)S(1)} copy(f32[64,256,32]{0,2,1:T(8,128)} %bitcast.22) | data formatting | bytes 4194304 | tf_op jit(solution)/shard_map/reshape | solution.py:26
  17.9 2.2 %fusion = f32[256,2048]{0,1:S(1)} fusion(f32[256,2048]{0,1:T(8,128)S(1)} %bitcast.23), kind=kOutput, calls=%fused_computation.5 | convolution fusion | flops 1612447744 | bytes 4194304
  20.1 1.9 %convolution_multiply_fusion = f32[64,256,32]{1,2,0:T(8,128)S(1)} fusion(f32[64,256,32]{1,2,0:T(8,128)S(1)} %bitcast.24), kind=kOutput, calls=%fused_computation.2 | convolution fusion | flops 201870336 | bytes 4194304 | tf_op jit(solution)/shard_map/cdb,be->cde/dot_general | solution.py:30
  22.0 4.5 %copy.15 = f32[64,256,32]{0,2,1:T(8,128)} copy(f32[64,256,32]{1,2,0:T(8,128)S(1)} %convolution_multiply_fusion) | data formatting | bytes 4194304 | tf_op jit(solution)/shard_map/div | solution.py:33
  26.5 7.6 %gather_fusion = f32[2048,64]{1,0:T(8,128)S(1)} fusion(f32[64,8192]{0,1:T(8,128)} %bitcast.21, s32[2048]{0:T(1024)S(1)} %get-tuple-element.7), kind=kCustom, calls=%fused_computation | custom fusion | bytes 1056768 | tf_op jit(solution)/shard_map/jit(_take)/gather | solution.py:46
  34.2 0.3 copy.16
  34.5 0.8 broadcast_select_fusion
  35.3 7.4 %all-to-all-start = ((f32[64,16,128]{2,0,1:T(8,128)}), f32[64,16,128]{2,0,1:T(8,128)S(1)}, u32[]{:S(2)}, u32[]{:S(2)}) async-start(f32[64,16,128]{2,0,1:T(8,128)} %broadcast_select_fusion), calls=%async_computation | async-start | bytes 1048576 | tf_op jit(solution)/shard_map/all_to_all | solution.py:48
  42.7 0.0 all-gather.3.cloned.1.call-start
  42.8 0.1 dynamic_slice.6
  42.9 14.1 %all-to-all-done = f32[64,16,128]{2,0,1:T(8,128)S(1)} async-done(((f32[64,16,128]{2,0,1:T(8,128)}), f32[64,16,128]{2,0,1:T(8,128)S(1)}, u32[]{:S(2)}, u32[]{:S(2)}) %all-to-all-start) | async-done | bytes 524320 | tf_op jit(solution)/shard_map/all_to_all | solution.py:48
  57.0 0.1 copy.20
  57.1 0.1 copy.19
  57.2 0.0 copy-start
  57.2 4.6 %all_gather.9 = f32[128,128]{1,0:T(8,128)S(1)} all-gather(f32[64,128]{1,0:T(8,128)S(1)} %copy.19), channel_id=1, replica_groups=mesh['row'=16,'col'=2] {'col'}, dimensions={0}, use_global_device_ids=true | all-gather | bytes 98304 | tf_op jit(solution)/shard_map/all_gather | solution.py:54
  61.8 0.9 fusion.81
  62.7 0.0 all-gather.3.cloned.1.call-update
  62.7 37.5 %all-gather.3.cloned.1.call-done = f32[2048,128]{1,0:T(8,128)} async-done(((f32[128,128]{1,0:T(8,128)}), f32[2048,128]{1,0:T(8,128)}) %all-gather.3.cloned.1.call-update) | async-done | bytes 1048592 | tf_op jit(solution)/shard_map/all_gather | solution.py:56
  100.2 1.3 %reduce_sum.19 = f32[128,128]{1,0:T(8,128)S(1)} reduce(f32[16,128,128]{2,1,0:T(8,128)} %bitcast.26, f32[]{:T(128)} %constant.76.clone.1), dimensions={0}, to_apply=%region_1.2 | reduce | flops 245760 | bytes 1114116 | tf_op jit(solution)/shard_map/reduce_sum | solution.py:57
  101.5 0.6 dynamic-slice_multiply_fusion
  102.1 0.0 copy-done
  (3 shorter events, 0.1 us)
Async XLA Ops:
  35.3 21.7 %all-to-all-start = ((f32[64,16,128]{2,0,1:T(8,128)}), f32[64,16,128]{2,0,1:T(8,128)S(1)}, u32[]{:S(2)}, u32[]{:S(2)}) async-start(f32[64,16,128]{2,0,1:T(8,128)} %broadcast_select_fusion), calls=%async_computation | async-start | bytes 1048576 | tf_op jit(solution)/shard_map/all_to_all | solution.py:48
  42.7 57.5 %all-gather.3.cloned.1.call-start = ((), (), s32[]{:S(2)}) async-start(), calls=%async_computation.1 | async-start | bytes 1114112 | tf_op jit(solution)/shard_map/all_gather | solution.py:56
  57.2 44.9 %copy-start = (f32[64,128]{1,0:T(8,128)}, f32[64,128]{1,0:T(8,128)S(1)}, u32[]{:S(2)}) copy-start(f32[64,128]{1,0:T(8,128)S(1)} %copy.19) | copy-start | bytes 98308
Sparse Core Ops, SparseCore 0:
  62.9 37.3 all-gather.2

commit v2 on v0

--- a/solution.py
+++ b/solution.py
@@ -45,7 +45,10 @@
     offset = sample_rows - owner * length
     chosen = jnp.take(mixed, offset, axis=1)
     pieces = chosen.reshape(columns, devices, per_device)
-    received = lax.all_to_all(pieces, "row", split_axis=1, concat_axis=1, tiled=True)
+    count = lax.axis_size("row")
+    shards = jnp.stack(jnp.split(pieces, count, axis=1), axis=0)
+    shards = lax.all_to_all(shards, "row", split_axis=0, concat_axis=0)
+    received = jnp.concatenate(shards, axis=1)
     mine = lax.dynamic_slice_in_dim(owner, position * per_device, per_device, 0)
     sources = jnp.arange(devices, dtype=jnp.int32)
     table = parity_sign(sources[:, None], mine[None, :], bit_count)

time: 158 us -> 167 us (1.057)
  local copies, waits for them, and re-layouts: 19.9 us -> 29.5 us
    unnamed x4 -> x19, local copies, waits for them, and re-layouts: 0.17 us -> 9.24 us
where the time goes in v2:
time: 167 us
  waiting for transfers between devices  102 us (61%)
  local copies, waits for them, and re-layouts  29.5 us (18%)
  between operations  14.1 us (8%)
  starting transfers between devices  6.3 us (4%)
  other arithmetic  5.08 us (3%)
  matrix products  4.98 us (3%)
  blocking collectives  4.71 us (3%)
    psum x1, waiting for transfers between devices, body(): totals = lax.psum(partial_gram, 'row')  88.7 us
    all_to_all x1, waiting for transfers between devices, body(): shards = lax.all_to_all(shards, 'row', split_axis=0, concat_axis=0)  13.3 us
    unnamed x19, local copies, waits for them, and re-layouts  9.24 us
    gather x2, local copies, waits for them, and re-layouts, body(): chosen = jnp.take(mixed, offset, axis=1)  7.96 us
    all_to_all x1, starting transfers between devices, body(): shards = lax.all_to_all(shards, 'row', split_axis=0, concat_axis=0)  6.27 us
    all_gather x1, blocking collectives, body(): gathered = lax.all_gather(sketch, 'col', axis=0, tiled=True)  4.71 us
    div x1, local copies, waits for them, and re-layouts, local_mix(): return values.reshape(columns, length) / jnp.sqrt(jnp.float32(length))  4.48 us
    reshape x1, local copies, waits for them, and re-layouts, local_mix(): values = values.reshape(columns, first_size, second_size)  4.46 us
  transfers between devices with their start and end apart: 2, of which 2 were waited for; matrix products, arithmetic and copies ran while one was open for 0% of the time, Pallas kernels for 0%

profile of v2, /device:TPU:8, one launch (start us, length us, event | category | flops | bytes accessed | tf_op | source)
XLA Modules:
  0.0 166.7 jit_solution(5680392664026605124)
XLA Ops:
  7.2 0.7 add_select_fusion
  7.9 0.7 and_bitcast_fusion
  8.6 0.8 convert_element_type.21
  9.4 1.4 convert_multiply_fusion
  10.8 2.7 %copy.13 = f32[64,8192]{0,1:T(8,128)} copy(f32[64,8192]{1,0:T(8,128)S(1)} %convert_multiply_fusion) | data formatting | bytes 4194304 | tf_op jit(solution)/shard_map/mul | solution.py:25
  13.5 4.5 %copy.14 = f32[64,256,32]{1,2,0:T(8,128)S(1)} copy(f32[64,256,32]{0,2,1:T(8,128)} %bitcast.91) | data formatting | bytes 4194304 | tf_op jit(solution)/shard_map/reshape | solution.py:26
  17.9 2.2 %fusion.1 = f32[256,2048]{0,1:S(1)} fusion(f32[256,2048]{0,1:T(8,128)S(1)} %bitcast.92), kind=kOutput, calls=%fused_computation.6 | convolution fusion | flops 1612447744 | bytes 4194304
  20.1 1.9 %convolution_multiply_fusion = f32[64,256,32]{1,2,0:T(8,128)S(1)} fusion(f32[64,256,32]{1,2,0:T(8,128)S(1)} %bitcast.93), kind=kOutput, calls=%fused_computation.2 | convolution fusion | flops 201870336 | bytes 4194304 | tf_op jit(solution)/shard_map/cdb,be->cde/dot_general | solution.py:30
  22.0 4.5 %copy.15 = f32[64,256,32]{0,2,1:T(8,128)} copy(f32[64,256,32]{1,2,0:T(8,128)S(1)} %convolution_multiply_fusion) | data formatting | bytes 4194304 | tf_op jit(solution)/shard_map/div | solution.py:33
  26.5 7.6 %gather_fusion = f32[2048,64]{1,0:T(8,128)S(1)} fusion(f32[64,8192]{0,1:T(8,128)} %bitcast.90, s32[2048]{0:T(1024)S(1)} %get-tuple-element.7), kind=kCustom, calls=%fused_computation | custom fusion | bytes 1056768 | tf_op jit(solution)/shard_map/jit(_take)/gather | solution.py:46
  34.2 0.3 copy.16
  34.5 0.6 fusion.55
  35.2 0.6 fusion.54
  35.8 0.6 fusion.53
  36.4 0.6 fusion.52
  37.0 0.6 fusion.51
  37.6 0.6 fusion.50
  38.2 0.6 fusion.49
  38.8 0.6 fusion.48
  39.4 0.6 fusion.47
  40.0 0.6 fusion.46
  40.6 0.6 fusion.45
  41.2 0.6 fusion.44
  41.8 0.6 fusion.43
  42.4 0.6 fusion.42
  43.0 0.6 fusion.41
  43.6 0.6 fusion.40
  44.2 6.3 %all-to-all-start = ((f32[16,64,1,128]{3,1,2,0:T(8,128)}), f32[16,64,1,128]{3,1,2,0:T(8,128)S(1)}, u32[]{:S(2)}, u32[]{:S(2)}) async-start(f32[16,64,1,128]{3,1,2,0:T(8,128)} %fusion.40), calls=%async_computation | async-start | bytes 1048576 | tf_op jit(solution)/shard_map/all_to_all | solution.py:50
  50.5 0.0 all-reduce.2.cloned.1.call-start
  50.6 0.1 dynamic_slice.6
  50.7 13.3 %all-to-all-done = f32[16,64,1,128]{3,1,2,0:T(8,128)S(1)} async-done(((f32[16,64,1,128]{3,1,2,0:T(8,128)}), f32[16,64,1,128]{3,1,2,0:T(8,128)S(1)}, u32[]{:S(2)}, u32[]{:S(2)}) %all-to-all-start) | async-done | bytes 524320 | tf_op jit(solution)/shard_map/all_to_all | solution.py:50
  64.0 0.1 copy.20
  64.2 0.1 copy.19
  64.2 0.0 copy-start
  64.2 4.7 %all_gather.3 = f32[128,128]{1,0:T(8,128)S(1)} all-gather(f32[64,128]{1,0:T(8,128)S(1)} %copy.19), channel_id=1, replica_groups=mesh['row'=16,'col'=2] {'col'}, dimensions={0}, use_global_device_ids=true | all-gather | bytes 98304 | tf_op jit(solution)/shard_map/all_gather | solution.py:57
  68.9 0.9 fusion.98
  69.8 0.0 all-reduce.2.cloned.1.call-update
  69.9 88.7 %all-reduce.2.cloned.1.call-done = f32[128,128]{1,0:T(8,128)} async-done(((f32[128,128]{1,0:T(8,128)}), f32[128,128]{1,0:T(8,128)}) %all-reduce.2.cloned.1.call-update) | async-done | bytes 65552 | tf_op jit(solution)/shard_map/psum | solution.py:59
  158.5 1.4 dynamic-slice_multiply_fusion
  159.9 0.0 copy-done
  (4 shorter events, 0.1 us)
Async XLA Ops:
  44.2 19.8 %all-to-all-start = ((f32[16,64,1,128]{3,1,2,0:T(8,128)}), f32[16,64,1,128]{3,1,2,0:T(8,128)S(1)}, u32[]{:S(2)}, u32[]{:S(2)}) async-start(f32[16,64,1,128]{3,1,2,0:T(8,128)} %fusion.40), calls=%async_computation | async-start | bytes 1048576 | tf_op jit(solution)/shard_map/all_to_all | solution.py:50
  50.5 108.0 %all-reduce.2.cloned.1.call-start = ((), (), s32[]{:S(2)}) async-start(), calls=%async_computation.1 | async-start | bytes 131072 | tf_op jit(solution)/shard_map/psum | solution.py:59
  64.2 95.7 %copy-start = (f32[64,128]{1,0:T(8,128)}, f32[64,128]{1,0:T(8,128)S(1)}, u32[]{:S(2)}) copy-start(f32[64,128]{1,0:T(8,128)S(1)} %copy.19) | copy-start | bytes 98308
Sparse Core Ops, SparseCore 0:
  70.0 88.5 all-reduce.1
